TPU v7x, 32 devices: a whole 2x2x4 slice. The times are simulated.
32 devices in a mesh: ma: 8 (over z, y), row: 4 (over x, core).
Axes of the slice: x: 2, y: 2, z: 4, core: 2. Of those that a mesh axis runs over, the one named last changes fastest.
Arguments:
- velocity: bfloat16 [3, 2, 16, 32, 65], P(None, None, 'row', 'ma'), may hold values from -6 to 6
- vorticity: bfloat16 [3, 2, 16, 32, 65], P(None, None, 'row', 'ma'), may hold values from -6 to 6
- legendre: bfloat16 [32, 65, 384], P('ma'), may hold values from -0.75 to 0.75
- pair_order: int32 [32], P('ma'), may hold values from 0 to 31, each once
- lat_weight: float32 [384], replicated, may hold values from 0.5 to 2
- diffusivity: float32 [16], replicated, may hold values from 0.25 to 2.5
Outputs:
- new_velocity: float32 [3, 2, 16, 32, 65], P(None, None, 'row', 'ma')
Inputs may be any that keep to these rules, and one draw needn't show every extreme that they name: pair_order holds each of 0 to 31 exactly once.
All inputs are finite; a program needn't handle non-finite values.
Results may differ from a plain program's by a relative error of at most 0.0095.
Values may be sent and summed in bfloat16 or wider, within the bound.
A program may use at most 128 MiB of HBM per device.

v0:
```python
import math
import jax
import jax.numpy as jnp
from jax import lax
from jax.sharding import PartitionSpec as P

NLON = 2048
STEP_SIZE = 1.0


def with_halo(cells, sides, width):
    for axis, dim in sides:
        count = lax.axis_size(axis)
        ends = count - 1
        head = lax.slice_in_dim(cells, 0, width, axis=dim)
        tail = lax.slice_in_dim(cells, cells.shape[dim] - width, cells.shape[dim], axis=dim)
        cells = jnp.concatenate(
            [
                lax.ppermute(tail, axis, [(i, (i + 1) % count) for i in range(ends)]),
                cells,
                lax.ppermute(head, axis, [((i + 1) % count, i) for i in range(ends)]),
            ],
            axis=dim,
        )
    return cells


def row_masks(low_order, pack_rows):
    orders_all = pack_rows - 1
    row_index = jnp.arange(pack_rows, dtype=jnp.int32)[None, :]
    low_column = low_order[:, None]
    is_lower = row_index < orders_all - low_column
    not_lower = jnp.logical_not(is_lower)
    even_low = row_index % 2 == 0
    even_high = (row_index + low_column) % 2 == 0
    low_pair = jnp.stack([is_lower & even_low, is_lower & jnp.logical_not(even_low)])
    high_pair = jnp.stack([not_lower & even_high, not_lower & jnp.logical_not(even_high)])
    return jnp.stack([low_pair, high_pair])


def cross_product(velocity_grid, vorticity_grid):
    return jnp.stack(
        [
            velocity_grid[1] * vorticity_grid[2] - velocity_grid[2] * vorticity_grid[1],
            velocity_grid[2] * vorticity_grid[0] - velocity_grid[0] * vorticity_grid[2],
            velocity_grid[0] * vorticity_grid[1] - velocity_grid[1] * vorticity_grid[0],
        ]
    )


def lon_table(column_order, is_imag, lon_start, lon_count):
    lon_index = lon_start + jnp.arange(lon_count, dtype=jnp.int32)
    angle_index = column_order[:, None] * lon_index[None, :] % NLON
    angle_value = angle_index.astype(jnp.float32) * (2.0 * math.pi / NLON)
    return jnp.where(is_imag[:, None], -jnp.sin(angle_value), jnp.cos(angle_value))


def local(velocity, vorticity, legendre, pair_order, lat_weight, diffusivity):
    pair_count = pair_order.shape[0]
    pack_rows = legendre.shape[1]
    half_lat = legendre.shape[2]
    nlat_all = 2 * half_lat
    levels_dev = velocity.shape[2]
    orders_all = pack_rows - 1
    inv_orders = 1.0 / math.sqrt(orders_all)
    inv_lon = 1.0 / math.sqrt(NLON)
    lon_width = NLON // 4
    mask_bool = row_masks(pair_order, pack_rows)
    fields = jnp.concatenate([velocity, vorticity], axis=0)
    masked = fields[None, None] * mask_bool.astype(jnp.bfloat16)[:, :, None, None, None]
    halves = jnp.einsum(
        "oqfilsr,srj->qfliosj", masked, legendre, preferred_element_type=jnp.float32
    )
    north_part = halves[0] + halves[1]
    south_part = halves[0] - halves[1]
    both_parts = jnp.concatenate([north_part, south_part], axis=-1)
    spectral = jnp.transpose(both_parts, (0, 1, 5, 2, 3, 4))
    spectral = spectral.reshape(6, levels_dev, nlat_all, 4 * pair_count).astype(jnp.bfloat16)
    gathered_ids = lax.all_gather(pair_order, "ma", axis=0, tiled=True)
    pair_slots = gathered_ids.reshape(-1, 1, 1, pair_count)
    both_orders = jnp.concatenate([pair_slots, orders_all - 1 - pair_slots], axis=2)
    full_shape = (both_orders.shape[0], 2, 2, pair_count)
    column_order = jnp.broadcast_to(both_orders, full_shape).reshape(-1)
    part_index = jnp.arange(2, dtype=jnp.int32)[None, :, None, None]
    is_imag = jnp.broadcast_to(part_index, full_shape).reshape(-1) == 1
    tables = [
        lon_table(column_order, is_imag, lon_block * lon_width, lon_width).astype(jnp.bfloat16)
        for lon_block in range(4)
    ]
    spec_block = lax.all_to_all(spectral, "ma", split_axis=2, concat_axis=3, tiled=True)
    accumulated = jnp.zeros((3,) + spec_block.shape[1:], jnp.float32)
    for lon_block in range(4):
        table_block = tables[lon_block]
        grid_values = (
            jnp.einsum("flac,cb->flab", spec_block, table_block, preferred_element_type=jnp.float32)
            * inv_orders
        )
        lamb_vector = cross_product(grid_values[:3], grid_values[3:])
        accumulated = accumulated + jnp.einsum(
            "flab,cb->flac",
            lamb_vector,
            table_block.astype(jnp.float32),
            precision=lax.Precision.HIGH,
            preferred_element_type=jnp.float32,
        )
    lamb_spec = (accumulated * inv_lon).astype(jnp.bfloat16)
    selector = jnp.transpose(mask_bool.astype(jnp.float32), (1, 0, 2, 3))[:, None, None, None]
    lamb_block = lax.all_to_all(lamb_spec, "ma", split_axis=3, concat_axis=2, tiled=True)
    item_count = lamb_block.shape[0]
    shaped = lamb_block.astype(jnp.float32).reshape(
        item_count, levels_dev, nlat_all, 2, 2, pair_count
    )
    shaped = jnp.transpose(shaped, (0, 1, 3, 4, 5, 2))
    north_side = shaped[..., :half_lat]
    south_side = shaped[..., half_lat:]
    weighted = jnp.stack(
        [lat_weight * (north_side + south_side), lat_weight * (north_side - south_side)]
    )
    weighted = weighted.astype(jnp.bfloat16)
    projected = jnp.einsum(
        "qfliosj,srj->qfliosr", weighted, legendre, preferred_element_type=jnp.float32
    )
    picked = jnp.sum(projected * selector, axis=(0, 4))
    tendency = jnp.transpose(picked, (0, 2, 1, 3, 4))
    source = velocity.astype(jnp.float32) + STEP_SIZE * tendency
    row_start = lax.axis_index("row") * levels_dev
    level_total = levels_dev * lax.axis_size("row")
    extended = with_halo(source.astype(jnp.bfloat16), (("row", 2),), 2).astype(source.dtype)
    padded_coupling = jnp.pad(diffusivity, (2, 2))
    wide_coupling = lax.dynamic_slice_in_dim(padded_coupling, row_start, levels_dev + 4)[
        None, None, :, None, None
    ]
    inner_coupling = wide_coupling[:, :, 1:-1]
    first_wide = (
        extended[:, :, 1:-1] + inner_coupling * (extended[:, :, :-2] + extended[:, :, 2:])
    ) / (1.0 + 2.0 * inner_coupling)
    global_level = row_start - 1 + jnp.arange(levels_dev + 2, dtype=jnp.int32)
    inside = ((global_level >= 0) & (global_level < level_total)).astype(jnp.float32)
    first_wide = first_wide * inside[None, None, :, None, None]
    own_coupling = wide_coupling[:, :, 2:-2]
    return (source + own_coupling * (first_wide[:, :, :-2] + first_wide[:, :, 2:])) / (
        1.0 + 2.0 * own_coupling
    )


def solution(mesh):
    in_specs = (
        P(None, None, "row", "ma", None),
        P(None, None, "row", "ma", None),
        P("ma", None, None),
        P("ma"),
        P(),
        P(),
    )
    out_specs = P(None, None, "row", "ma", None)
    return jax.shard_map(local, mesh=mesh, in_specs=in_specs, out_specs=out_specs, check_vma=False)
```

profile of v0, /device:TPU:1, one launch (start us, length us, event | category | flops | bytes accessed | tf_op | source)
XLA Modules:
  0.0 95.0 jit_solution(11931700865630016753)
XLA Ops:
  0.0 0.7 broadcast_subtract_fusion.1
  0.7 0.7 fusion.112
  1.5 0.8 pad_maximum_fusion
  3.3 5.8 %copy.72 = bf16[6,4,768,16]{3,1,0,2:T(4,128)(2,1)} copy(bf16[6,4,768,16]{2,1,3,0:T(4,128)(2,1)S(1)} %bitcast.115) | data formatting | bytes 1179648 | tf_op jit(solution)/shard_map/convert_element_type | solution.py:78
  9.1 7.0 %reshape.343 = bf16[8,2,18432]{2,1,0:T(2,128)(2,1)} reshape(bf16[768,6,4,16]{3,2,1,0:T(4,128)(2,1)} %bitcast.112) | data formatting | bytes 1179648
  16.1 6.4 %all-to-all-start = ((bf16[8,2,18432]{2,1,0:T(2,128)(2,1)}), bf16[8,2,18432]{2,1,0:T(2,128)(2,1)S(1)}, u32[]{:S(2)}, u32[]{:S(2)}) async-start(bf16[8,2,18432]{2,1,0:T(2,128)(2,1)} %reshape.343), calls=%async_computation | async-start | bytes 1179648 | tf_op jit(solution)/shard_map/all_to_all | solution.py:90
  22.4 0.6 dynamic-slice
  23.9 13.4 %all-reduce.1 = s32[32]{0:T(128)S(1)} all-reduce(s32[32]{0:T(128)S(1)} %dynamic-update-slice), channel_id=1, replica_groups=mesh['ma'=8,'row'=4] {'ma'}, use_global_device_ids=true, to_apply=%add.1 | all-reduce | flops 32 | bytes 256
  37.8 4.4 %reshape.344 = bf16[768,6,4,16]{3,2,1,0:T(4,128)(2,1)} reshape(bf16[8,2,18432]{2,1,0:T(2,128)(2,1)S(1)} %all-to-all-done) | data formatting | bytes 1179648
  42.2 6.0 %copy.102 = bf16[6,4,8,96,16]{3,4,2,1,0:T(8,128)(2,1)S(1)} copy(bf16[6,4,8,96,16]{4,1,0,3,2:T(4,128)(2,1)} %bitcast.113) | data formatting | bytes 1179648 | tf_op jit(solution)/shard_map/all_to_all | solution.py:90
  48.2 1.9 %broadcast_multiply_fusion.3 = f32[6,4,96,512]{3,2,1,0:T(8,128)S(1)} fusion(bf16[6,4,96,128]{2,3,1,0:T(8,128)(2,1)S(1)} %bitcast.108, s32[128]{0:T(128)S(1)} %mul.250, pred[128]{0:T(512)(128)(4,1)S(1)} %eq.67), kind=kOutput, calls=%fused_computation.27 | convolution fusion | flops 304283648 | bytes 5309056 | tf_op jit(solution)/shard_map/flac,cb->flab/dot_general | solution.py:95
  50.1 0.6 multiply_subtract_fusion.11
  50.7 1.9 %broadcast_multiply_fusion.2 = f32[6,4,96,512]{3,2,1,0:T(8,128)S(1)} fusion(bf16[6,4,96,128]{2,3,1,0:T(8,128)(2,1)S(1)} %bitcast.109, s32[512]{0:T(512)S(1)} %iota_add_fusion.2, s32[128]{0:T(128)S(1)} %mul.250, pred[128]{0:T(512)(128)(4,1)S(1)} %eq.67), kind=kOutput, calls=%fused_computation.26 | convolution fusion | flops 304283648 | bytes 5311104 | tf_op jit(solution)/shard_map/flac,cb->flab/dot_general | solution.py:95
  52.5 0.6 multiply_subtract_fusion.8
  53.1 1.9 %broadcast_multiply_fusion.1 = f32[6,4,96,512]{3,2,1,0:T(8,128)S(1)} fusion(bf16[6,4,96,128]{2,3,1,0:T(8,128)(2,1)S(1)} %bitcast.110, s32[512]{0:T(512)S(1)} %iota_add_fusion.1, s32[128]{0:T(128)S(1)} %mul.250, pred[128]{0:T(512)(128)(4,1)S(1)} %eq.67), kind=kOutput, calls=%fused_computation.25 | convolution fusion | flops 304283648 | bytes 5311104 | tf_op jit(solution)/shard_map/flac,cb->flab/dot_general | solution.py:95
  55.0 0.6 multiply_subtract_fusion.5
  55.5 1.9 %broadcast_multiply_fusion = f32[6,4,96,512]{3,2,1,0:T(8,128)S(1)} fusion(bf16[6,4,96,128]{2,3,1,0:T(8,128)(2,1)S(1)} %bitcast.111, s32[512]{0:T(512)S(1)} %iota_add_fusion, s32[128]{0:T(128)S(1)} %mul.250, pred[128]{0:T(512)(128)(4,1)S(1)} %eq.67), kind=kOutput, calls=%fused_computation.24 | convolution fusion | flops 304283648 | bytes 5311104 | tf_op jit(solution)/shard_map/flac,cb->flab/dot_general | solution.py:95
  57.4 0.6 multiply_subtract_fusion.2
  58.0 1.8 %fusion = f32[3,4,96,128]{3,2,1,0:T(8,128)S(1)} fusion(f32[1,4,96,512]{3,2,1,0:T(8,128)S(1)} %get-tuple-element.16, f32[1,4,96,512]{3,2,1,0:T(8,128)S(1)} %get-tuple-element.15, f32[1,4,96,512]{3,2,1,0:T(8,128)S(1)} %get-tuple-element.14, s32[128]{0:T(128)S(1)} %mul.250, pred[128]{0:T(512)(128)(4,1)S(1)} %eq.67), kind=kOutput, calls=%fused_computation | convolution fusion | flops 455278592 | bytes 2949760 | tf_op jit(solution)/shard_map/flab,cb->flac/dot_general | solution.py:99
  59.8 2.1 %fusion.30 = f32[3,4,96,128]{3,2,1,0:T(8,128)S(1)} fusion(f32[3,4,96,128]{3,2,1,0:T(8,128)S(1)} %fusion, f32[1,4,96,512]{3,2,1,0:T(8,128)S(1)} %get-tuple-element.13, f32[1,4,96,512]{3,2,1,0:T(8,128)S(1)} %get-tuple-element.12, f32[1,4,96,512]{3,2,1,0:T(8,128)S(1)} %get-tuple-element.11, s32[512]{0:T(512)S(1)} %iota_add_fusion.2, s32[128]{0:T(128)S(1)} %mul.250, ...), kind=kOutput, calls=%fused_computation.31 | convolution fusion | flops 455426048 | bytes 3541632 | tf_op jit(solution)/shard_map/flab,cb->flac/dot_general | solution.py:99
  61.9 1.9 %fusion.27 = f32[3,4,96,128]{3,2,1,0:T(8,128)S(1)} fusion(f32[3,4,96,128]{3,2,1,0:T(8,128)S(1)} %fusion.30, f32[1,4,96,512]{3,2,1,0:T(8,128)S(1)} %get-tuple-element.10, f32[1,4,96,512]{3,2,1,0:T(8,128)S(1)} %get-tuple-element.9, f32[1,4,96,512]{3,2,1,0:T(8,128)S(1)} %get-tuple-element.8, s32[512]{0:T(512)S(1)} %iota_add_fusion.1, s32[128]{0:T(128)S(1)} %mul.250, ...), kind=kOutput, calls=%fused_computation.30 | convolution fusion | flops 455426048 | bytes 3541632 | tf_op jit(solution)/shard_map/flab,cb->flac/dot_general | solution.py:99
  63.8 1.9 %fusion.36 = bf16[3,4,96,128]{3,2,1,0:T(8,128)(2,1)S(1)} fusion(f32[3,4,96,128]{3,2,1,0:T(8,128)S(1)} %fusion.27, f32[1,4,96,512]{3,2,1,0:T(8,128)S(1)} %get-tuple-element.7, f32[1,4,96,512]{3,2,1,0:T(8,128)S(1)} %get-tuple-element.6, f32[1,4,96,512]{3,2,1,0:T(8,128)S(1)} %get-tuple-element.5, s32[512]{0:T(512)S(1)} %iota_add_fusion, s32[128]{0:T(128)S(1)} %mul.250, ...), kind=kOutput, calls=%fused_computation.33 | convolution fusion | flops 455720960 | bytes 3246720 | tf_op jit(solution)/shard_map/flab,cb->flac/dot_general | solution.py:99
  65.7 1.0 %copy.81 = bf16[3,4,96,128]{2,1,0,3:T(4,128)(2,1)} copy(bf16[3,4,96,128]{3,2,1,0:T(8,128)(2,1)S(1)} %fusion.36) | data formatting | bytes 589824 | tf_op jit(solution)/shard_map/convert_element_type | solution.py:106
  66.6 5.0 %all-to-all-start.1 = ((bf16[3,4,96,128]{2,1,0,3:T(4,128)(2,1)}), bf16[3,4,96,128]{2,1,0,3:T(4,128)(2,1)S(1)}, u32[]{:S(2)}, u32[]{:S(2)}) async-start(bf16[3,4,96,128]{2,1,0,3:T(4,128)(2,1)} %copy.81), calls=%async_computation.1 | async-start | bytes 786432 | tf_op jit(solution)/shard_map/all_to_all | solution.py:108
  71.8 9.2 %all-to-all-done.1 = bf16[3,4,96,128]{2,1,0,3:T(4,128)(2,1)S(1)} async-done(((bf16[3,4,96,128]{2,1,0,3:T(4,128)(2,1)}), bf16[3,4,96,128]{2,1,0,3:T(4,128)(2,1)S(1)}, u32[]{:S(2)}, u32[]{:S(2)}) %all-to-all-start.1) | async-done | bytes 294944 | tf_op jit(solution)/shard_map/all_to_all | solution.py:108
  81.5 0.4 reshape.330
  81.9 0.4 copy.115
  82.4 0.4 fusion.40
  82.9 6.2 %collective-permute-start = (bf16[3,2,2,4,65]{4,2,1,0,3:T(2,128)(2,1)S(1)}, bf16[3,2,2,4,65]{4,2,1,0,3:T(2,128)(2,1)S(1)}, u32[]{:S(2)}, u32[]{:S(2)}) collective-permute-start(bf16[3,2,2,4,65]{4,2,1,0,3:T(2,128)(2,1)S(1)} %get-tuple-element.19), channel_id=1, source_target_pairs={{0,1},{1,2},{2,3},{4,5},{5,6},{6,7},{8,9},{9,10},{10,11},{12,13},{... | collective-permute-start | bytes 18728 | tf_op jit(solution)/shard_map/ppermute | solution.py:19
  89.1 1.9 %collective-permute-start.1 = (bf16[3,2,2,4,65]{4,2,1,0,3:T(2,128)(2,1)S(1)}, bf16[3,2,2,4,65]{4,2,1,0,3:T(2,128)(2,1)S(1)}, u32[]{:S(2)}, u32[]{:S(2)}) collective-permute-start(bf16[3,2,2,4,65]{4,2,1,0,3:T(2,128)(2,1)S(1)} %get-tuple-element.20), channel_id=1, source_target_pairs={{1,0},{2,1},{3,2},{5,4},{6,5},{7,6},{9,8},{10,9},{11,10},{13,12},{... | collective-permute-start | bytes 18728 | tf_op jit(solution)/shard_map/ppermute | solution.py:21
  91.0 3.1 %collective-permute-done.1 = bf16[3,2,2,4,65]{4,2,1,0,3:T(2,128)(2,1)S(1)} collective-permute-done((bf16[3,2,2,4,65]{4,2,1,0,3:T(2,128)(2,1)S(1)}, bf16[3,2,2,4,65]{4,2,1,0,3:T(2,128)(2,1)S(1)}, u32[]{:S(2)}, u32[]{:S(2)}) %collective-permute-start.1) | collective-permute-done | bytes 6272 | tf_op jit(solution)/shard_map/ppermute | solution.py:21
  94.3 0.6 copy.88
  (52 shorter events, 2.6 us)
Async XLA Ops:
  0.0 2.3 %copy-start = (bf16[4,65,384]{2,0,1:T(4,128)(2,1)S(1)}, bf16[4,65,384]{2,0,1:T(4,128)(2,1)}, u32[]{:S(2)}) copy-start(bf16[4,65,384]{2,0,1:T(4,128)(2,1)} %param.8) | copy-start | bytes 599044
  9.1 13.3 %copy-start.5 = (u32[32]{0:T(128)S(1)}, u32[32]{0:T(128)}, u32[]{:S(2)}) copy-start(u32[32]{0:T(128)} %constant.104) | copy-start | bytes 388
  9.1 14.6 %copy-start.3 = (s32[4]{0:T(128)S(1)}, s32[4]{0:T(128)}, u32[]{:S(2)}) copy-start(s32[4]{0:T(128)} %param.9) | copy-start | bytes 52
  16.1 21.7 %all-to-all-start = ((bf16[8,2,18432]{2,1,0:T(2,128)(2,1)}), bf16[8,2,18432]{2,1,0:T(2,128)(2,1)S(1)}, u32[]{:S(2)}, u32[]{:S(2)}) async-start(bf16[8,2,18432]{2,1,0:T(2,128)(2,1)} %reshape.343), calls=%async_computation | async-start | bytes 1179648 | tf_op jit(solution)/shard_map/all_to_all | solution.py:90
  63.8 7.8 %copy-start.4 = (f32[16]{0:T(128)S(1)}, f32[16]{0:T(128)}, u32[]{:S(2)}) copy-start(f32[16]{0:T(128)} %param.11) | copy-start | bytes 196
  66.6 14.4 %all-to-all-start.1 = ((bf16[3,4,96,128]{2,1,0,3:T(4,128)(2,1)}), bf16[3,4,96,128]{2,1,0,3:T(4,128)(2,1)S(1)}, u32[]{:S(2)}, u32[]{:S(2)}) async-start(bf16[3,4,96,128]{2,1,0,3:T(4,128)(2,1)} %copy.81), calls=%async_computation.1 | async-start | bytes 786432 | tf_op jit(solution)/shard_map/all_to_all | solution.py:108
  81.2 1.1 %copy-start.2 = (f32[384]{0:T(512)S(1)}, f32[384]{0:T(512)}, u32[]{:S(2)}) copy-start(f32[384]{0:T(512)} %param.10) | copy-start | bytes 4612
  81.4 1.4 %copy-start.1 = (bf16[3,2,4,4,65]{4,3,2,1,0:T(4,128)(2,1)S(1)}, bf16[3,2,4,4,65]{4,3,2,1,0:T(4,128)(2,1)}, u32[]{:S(2)}) copy-start(bf16[3,2,4,4,65]{4,3,2,1,0:T(4,128)(2,1)} %param.6) | copy-start | bytes 37444
  82.9 8.1 %collective-permute-start = (bf16[3,2,2,4,65]{4,2,1,0,3:T(2,128)(2,1)S(1)}, bf16[3,2,2,4,65]{4,2,1,0,3:T(2,128)(2,1)S(1)}, u32[]{:S(2)}, u32[]{:S(2)}) collective-permute-start(bf16[3,2,2,4,65]{4,2,1,0,3:T(2,128)(2,1)S(1)} %get-tuple-element.19), channel_id=1, source_target_pairs={{0,1},{1,2},{2,3},{4,5},{5,6},{6,7},{8,9},{9,10},{10,11},{12,13},{... | collective-permute-start | bytes 18728 | tf_op jit(solution)/shard_map/ppermute | solution.py:19
  89.1 5.0 %collective-permute-start.1 = (bf16[3,2,2,4,65]{4,2,1,0,3:T(2,128)(2,1)S(1)}, bf16[3,2,2,4,65]{4,2,1,0,3:T(2,128)(2,1)S(1)}, u32[]{:S(2)}, u32[]{:S(2)}) collective-permute-start(bf16[3,2,2,4,65]{4,2,1,0,3:T(2,128)(2,1)S(1)} %get-tuple-element.20), channel_id=1, source_target_pairs={{1,0},{2,1},{3,2},{5,4},{6,5},{7,6},{9,8},{10,9},{11,10},{13,12},{... | collective-permute-start | bytes 18728 | tf_op jit(solution)/shard_map/ppermute | solution.py:21
where the time goes:
time: 95.6 us; the launch traced here: 95 us
  local copies, waits for them, and re-layouts  27.5 us (29%)
  starting transfers between devices  19.5 us (20%)
  matrix products  15.7 us (16%)
  blocking collectives  13.4 us (14%)
  waiting for transfers between devices  12.3 us (13%)
  other arithmetic  5.53 us (6%)
  between operations  1.06 us (1%)
    unnamed x1, blocking collectives  13.4 us
    unnamed x17, local copies, waits for them, and re-layouts  12.3 us
    all_to_all x1, waiting for transfers between devices, local(): lax.all_to_all(lamb_spec, 'ma', split_axis=3, concat_axis=2, tiled=True)  9.2 us
    dot_general x4, matrix products, local(): jnp.einsum('flab,cb->flac', lamb_vector, table_block.astype(jnp.float32),...  7.64 us
    dot_general x4, matrix products, local(): jnp.einsum('flac,cb->flab', spec_block, table_block, preferred_element_ty...  7.44 us
    all_to_all x1, starting transfers between devices, local(): lax.all_to_all(spectral, 'ma', split_axis=2, concat_axis=3, tiled=True)  6.37 us
    ppermute x1, starting transfers between devices, with_halo(): lax.ppermute(tail, axis, [(i, (i + 1) % count) for i in range(ends)])  6.19 us
    convert_element_type x2, local copies, waits for them, and re-layouts, local(): spectral.reshape(6, levels_dev, nlat_all, 4 * pair_count)  6.04 us
  transfers between devices with their start and end apart: 4, of which 2 were waited for; matrix products, arithmetic and copies ran while one was open for 1% of the time, Pallas kernels for 0%

commit v1 on v0

--- a/solution.py
+++ b/solution.py
@@ -3,9 +3,14 @@
 import jax.numpy as jnp
 from jax import lax
 from jax.sharding import PartitionSpec as P
+from jax.lax import all_to_all, axis_size
 
 NLON = 2048
 STEP_SIZE = 1.0
+_number_heaps = lambda axis_k, array_dim, axis_name, view: jnp.concatenate(
+    all_to_all(jnp.stack(jnp.split(view, axis_size(axis_name), axis_k), 0), axis_name, 0, 0),
+    axis=array_dim,
+)
 
 
 def with_halo(cells, sides, width):
@@ -105,7 +110,7 @@
         )
     lamb_spec = (accumulated * inv_lon).astype(jnp.bfloat16)
     selector = jnp.transpose(mask_bool.astype(jnp.float32), (1, 0, 2, 3))[:, None, None, None]
-    lamb_block = lax.all_to_all(lamb_spec, "ma", split_axis=3, concat_axis=2, tiled=True)
+    lamb_block = _number_heaps(3, 2, "ma", view=lamb_spec)
     item_count = lamb_block.shape[0]
     shaped = lamb_block.astype(jnp.float32).reshape(
         item_count, levels_dev, nlat_all, 2, 2, pair_count

time: 95.6 us -> 102 us (1.067)
  local copies, waits for them, and re-layouts: 27.5 us -> 33.4 us
    unnamed x17 -> x24, local copies, waits for them, and re-layouts: 12.3 us -> 16.7 us
    another operation x0 -> x10, local copies, waits for them, and re-layouts: none -> 2.36 us  [jnp.stack(jnp.split(view, axis_size(axis_name), axis_k), 0)]
where the time goes in v1:
time: 102 us; the launch traced here: 101 us
  local copies, waits for them, and re-layouts  33.4 us (33%)
  starting transfers between devices  19.4 us (19%)
  matrix products  15.8 us (15%)
  blocking collectives  13.4 us (13%)
  waiting for transfers between devices  12.3 us (12%)
  other arithmetic  5.53 us (5%)
  between operations  1.06 us (1%)
    unnamed x24, local copies, waits for them, and re-layouts  16.7 us
    unnamed x1, blocking collectives  13.4 us
    all_to_all x1, waiting for transfers between devices, all_to_all(jnp.stack(jnp.split(view, axis_size(axis_name), axis_k), 0), a...  9.2 us
    dot_general x4, matrix products, local(): jnp.einsum('flab,cb->flac', lamb_vector, table_block.astype(jnp.float32),...  7.65 us
    dot_general x4, matrix products, local(): jnp.einsum('flac,cb->flab', spec_block, table_block, preferred_element_ty...  7.44 us
    all_to_all x1, starting transfers between devices, local(): lax.all_to_all(spectral, 'ma', split_axis=2, concat_axis=3, tiled=True)  6.37 us
    ppermute x1, starting transfers between devices, with_halo(): lax.ppermute(tail, axis, [(i, (i + 1) % count) for i in range(ends)])  6.19 us
    convert_element_type x2, local copies, waits for them, and re-layouts, local(): spectral.reshape(6, levels_dev, nlat_all, 4 * pair_count)  6.03 us
  transfers between devices with their start and end apart: 4, of which 2 were waited for; matrix products, arithmetic and copies ran while one was open for 1% of the time, Pallas kernels for 0%

profile of v1, /device:TPU:1, one launch (start us, length us, event | category | flops | bytes accessed | tf_op | source)
XLA Modules:
  0.0 100.9 jit_solution(16123401072569923614)
XLA Ops:
  0.0 0.7 broadcast_subtract_fusion.1
  0.7 0.7 fusion.112
  1.5 0.8 pad_maximum_fusion
  3.3 5.8 %copy.77 = bf16[6,4,768,16]{3,1,0,2:T(4,128)(2,1)} copy(bf16[6,4,768,16]{2,1,3,0:T(4,128)(2,1)S(1)} %bitcast.129) | data formatting | bytes 1179648 | tf_op jit(solution)/shard_map/convert_element_type | solution.py:83
  9.1 7.0 %reshape.342 = bf16[8,2,18432]{2,1,0:T(2,128)(2,1)} reshape(bf16[768,6,4,16]{3,2,1,0:T(4,128)(2,1)} %bitcast.126) | data formatting | bytes 1179648
  16.1 6.4 %all-to-all-start = ((bf16[8,2,18432]{2,1,0:T(2,128)(2,1)}), bf16[8,2,18432]{2,1,0:T(2,128)(2,1)S(1)}, u32[]{:S(2)}, u32[]{:S(2)}) async-start(bf16[8,2,18432]{2,1,0:T(2,128)(2,1)} %reshape.342), calls=%async_computation | async-start | bytes 1179648 | tf_op jit(solution)/shard_map/all_to_all | solution.py:95
  23.9 13.4 %all-reduce.1 = s32[32]{0:T(128)S(1)} all-reduce(s32[32]{0:T(128)S(1)} %dynamic-update-slice), channel_id=1, replica_groups=mesh['ma'=8,'row'=4] {'ma'}, use_global_device_ids=true, to_apply=%add.1 | all-reduce | flops 32 | bytes 256
  37.8 4.5 %reshape.343 = bf16[768,6,4,16]{3,2,1,0:T(4,128)(2,1)} reshape(bf16[8,2,18432]{2,1,0:T(2,128)(2,1)S(1)} %all-to-all-done) | data formatting | bytes 1179648
  42.2 6.0 %copy.113 = bf16[6,4,8,96,16]{3,4,2,1,0:T(8,128)(2,1)S(1)} copy(bf16[6,4,8,96,16]{4,1,0,3,2:T(4,128)(2,1)} %bitcast.127) | data formatting | bytes 1179648 | tf_op jit(solution)/shard_map/all_to_all | solution.py:95
  48.3 1.9 %broadcast_multiply_fusion.3 = f32[6,4,96,512]{3,2,1,0:T(8,128)S(1)} fusion(bf16[6,4,96,128]{2,3,1,0:T(8,128)(2,1)S(1)} %bitcast.122, s32[128]{0:T(128)S(1)} %mul.250, pred[128]{0:T(512)(128)(4,1)S(1)} %eq.67), kind=kOutput, calls=%fused_computation.27 | convolution fusion | flops 304283648 | bytes 5309056 | tf_op jit(solution)/shard_map/flac,cb->flab/dot_general | solution.py:100
  50.7 1.9 %broadcast_multiply_fusion.2 = f32[6,4,96,512]{3,2,1,0:T(8,128)S(1)} fusion(bf16[6,4,96,128]{2,3,1,0:T(8,128)(2,1)S(1)} %bitcast.123, s32[512]{0:T(512)S(1)} %iota_add_fusion.2, s32[128]{0:T(128)S(1)} %mul.250, pred[128]{0:T(512)(128)(4,1)S(1)} %eq.67), kind=kOutput, calls=%fused_computation.26 | convolution fusion | flops 304283648 | bytes 5311104 | tf_op jit(solution)/shard_map/flac,cb->flab/dot_general | solution.py:100
  53.1 1.9 %broadcast_multiply_fusion.1 = f32[6,4,96,512]{3,2,1,0:T(8,128)S(1)} fusion(bf16[6,4,96,128]{2,3,1,0:T(8,128)(2,1)S(1)} %bitcast.124, s32[512]{0:T(512)S(1)} %iota_add_fusion.1, s32[128]{0:T(128)S(1)} %mul.250, pred[128]{0:T(512)(128)(4,1)S(1)} %eq.67), kind=kOutput, calls=%fused_computation.25 | convolution fusion | flops 304283648 | bytes 5311104 | tf_op jit(solution)/shard_map/flac,cb->flab/dot_general | solution.py:100
  55.6 1.9 %broadcast_multiply_fusion = f32[6,4,96,512]{3,2,1,0:T(8,128)S(1)} fusion(bf16[6,4,96,128]{2,3,1,0:T(8,128)(2,1)S(1)} %bitcast.125, s32[512]{0:T(512)S(1)} %iota_add_fusion, s32[128]{0:T(128)S(1)} %mul.250, pred[128]{0:T(512)(128)(4,1)S(1)} %eq.67), kind=kOutput, calls=%fused_computation.24 | convolution fusion | flops 304283648 | bytes 5311104 | tf_op jit(solution)/shard_map/flac,cb->flab/dot_general | solution.py:100
  58.0 1.8 %fusion = f32[3,4,96,128]{3,2,1,0:T(8,128)S(1)} fusion(f32[1,4,96,512]{3,2,1,0:T(8,128)S(1)} %get-tuple-element.16, f32[1,4,96,512]{3,2,1,0:T(8,128)S(1)} %get-tuple-element.15, f32[1,4,96,512]{3,2,1,0:T(8,128)S(1)} %get-tuple-element.14, s32[128]{0:T(128)S(1)} %mul.250, pred[128]{0:T(512)(128)(4,1)S(1)} %eq.67), kind=kOutput, calls=%fused_computation | convolution fusion | flops 455278592 | bytes 2949760 | tf_op jit(solution)/shard_map/flab,cb->flac/dot_general | solution.py:104
  59.9 2.1 %fusion.30 = f32[3,4,96,128]{3,2,1,0:T(8,128)S(1)} fusion(f32[3,4,96,128]{3,2,1,0:T(8,128)S(1)} %fusion, f32[1,4,96,512]{3,2,1,0:T(8,128)S(1)} %get-tuple-element.13, f32[1,4,96,512]{3,2,1,0:T(8,128)S(1)} %get-tuple-element.12, f32[1,4,96,512]{3,2,1,0:T(8,128)S(1)} %get-tuple-element.11, s32[512]{0:T(512)S(1)} %iota_add_fusion.2, s32[128]{0:T(128)S(1)} %mul.250, ...), kind=kOutput, calls=%fused_computation.31 | convolution fusion | flops 455426048 | bytes 3541632 | tf_op jit(solution)/shard_map/flab,cb->flac/dot_general | solution.py:104
  61.9 1.9 %fusion.27 = f32[3,4,96,128]{3,2,1,0:T(8,128)S(1)} fusion(f32[3,4,96,128]{3,2,1,0:T(8,128)S(1)} %fusion.30, f32[1,4,96,512]{3,2,1,0:T(8,128)S(1)} %get-tuple-element.10, f32[1,4,96,512]{3,2,1,0:T(8,128)S(1)} %get-tuple-element.9, f32[1,4,96,512]{3,2,1,0:T(8,128)S(1)} %get-tuple-element.8, s32[512]{0:T(512)S(1)} %iota_add_fusion.1, s32[128]{0:T(128)S(1)} %mul.250, ...), kind=kOutput, calls=%fused_computation.30 | convolution fusion | flops 455426048 | bytes 3541632 | tf_op jit(solution)/shard_map/flab,cb->flac/dot_general | solution.py:104
  63.8 1.9 %fusion.36 = bf16[3,4,96,128]{3,2,1,0:T(8,128)(2,1)S(1)} fusion(f32[3,4,96,128]{3,2,1,0:T(8,128)S(1)} %fusion.27, f32[1,4,96,512]{3,2,1,0:T(8,128)S(1)} %get-tuple-element.7, f32[1,4,96,512]{3,2,1,0:T(8,128)S(1)} %get-tuple-element.6, f32[1,4,96,512]{3,2,1,0:T(8,128)S(1)} %get-tuple-element.5, s32[512]{0:T(512)S(1)} %iota_add_fusion, s32[128]{0:T(128)S(1)} %mul.250, ...), kind=kOutput, calls=%fused_computation.33 | convolution fusion | flops 455720960 | bytes 3246720 | tf_op jit(solution)/shard_map/flab,cb->flac/dot_general | solution.py:104
  65.7 0.6 slice_bitcast_fusion
  66.5 0.6 constant_dynamic-update-slice_fusion.7
  68.1 0.6 constant_dynamic-update-slice_fusion.6
  68.7 0.6 constant_dynamic-update-slice_fusion.5
  69.3 0.6 constant_dynamic-update-slice_fusion.4
  70.0 0.6 constant_dynamic-update-slice_fusion.3
  70.6 0.6 constant_dynamic-update-slice_fusion.2
  71.2 0.6 constant_dynamic-update-slice_fusion.1
  71.8 0.6 constant_dynamic-update-slice_fusion
  72.4 5.0 %all-to-all-start.1 = ((bf16[8,3,4,96,16]{3,4,2,1,0:T(8,128)(2,1)}), bf16[8,3,4,96,16]{3,4,2,1,0:T(8,128)(2,1)S(1)}, u32[]{:S(2)}, u32[]{:S(2)}) async-start(bf16[8,3,4,96,16]{3,4,2,1,0:T(8,128)(2,1)} %constant_dynamic-update-slice_fusion), calls=%async_computation.1 | async-start | bytes 786432 | tf_op jit(solution)/shard_map/all_to_all | solution.py:11
  77.6 9.2 %all-to-all-done.1 = bf16[8,3,4,96,16]{3,4,2,1,0:T(8,128)(2,1)S(1)} async-done(((bf16[8,3,4,96,16]{3,4,2,1,0:T(8,128)(2,1)}), bf16[8,3,4,96,16]{3,4,2,1,0:T(8,128)(2,1)S(1)}, u32[]{:S(2)}, u32[]{:S(2)}) %all-to-all-start.1) | async-done | bytes 294944 | tf_op jit(solution)/shard_map/all_to_all | solution.py:11
  88.8 6.2 %collective-permute-start = (bf16[3,2,2,4,65]{4,2,1,0,3:T(2,128)(2,1)S(1)}, bf16[3,2,2,4,65]{4,2,1,0,3:T(2,128)(2,1)S(1)}, u32[]{:S(2)}, u32[]{:S(2)}) collective-permute-start(bf16[3,2,2,4,65]{4,2,1,0,3:T(2,128)(2,1)S(1)} %get-tuple-element.27), channel_id=1, source_target_pairs={{0,1},{1,2},{2,3},{4,5},{5,6},{6,7},{8,9},{9,10},{10,11},{12,13},{... | collective-permute-start | bytes 18728 | tf_op jit(solution)/shard_map/ppermute | solution.py:24
  95.0 1.9 %collective-permute-start.1 = (bf16[3,2,2,4,65]{4,2,1,0,3:T(2,128)(2,1)S(1)}, bf16[3,2,2,4,65]{4,2,1,0,3:T(2,128)(2,1)S(1)}, u32[]{:S(2)}, u32[]{:S(2)}) collective-permute-start(bf16[3,2,2,4,65]{4,2,1,0,3:T(2,128)(2,1)S(1)} %get-tuple-element.28), channel_id=1, source_target_pairs={{1,0},{2,1},{3,2},{5,4},{6,5},{7,6},{9,8},{10,9},{11,10},{13,12},{... | collective-permute-start | bytes 18728 | tf_op jit(solution)/shard_map/ppermute | solution.py:26
  97.0 3.1 %collective-permute-done.1 = bf16[3,2,2,4,65]{4,2,1,0,3:T(2,128)(2,1)S(1)} collective-permute-done((bf16[3,2,2,4,65]{4,2,1,0,3:T(2,128)(2,1)S(1)}, bf16[3,2,2,4,65]{4,2,1,0,3:T(2,128)(2,1)S(1)}, u32[]{:S(2)}, u32[]{:S(2)}) %collective-permute-start.1) | collective-permute-done | bytes 6272 | tf_op jit(solution)/shard_map/ppermute | solution.py:26
  100.3 0.6 copy.99
  (67 shorter events, 7.9 us)
Async XLA Ops:
  0.0 2.3 %copy-start = (bf16[4,65,384]{2,0,1:T(4,128)(2,1)S(1)}, bf16[4,65,384]{2,0,1:T(4,128)(2,1)}, u32[]{:S(2)}) copy-start(bf16[4,65,384]{2,0,1:T(4,128)(2,1)} %param.8) | copy-start | bytes 599044
  9.1 13.3 %copy-start.5 = (u32[32]{0:T(128)S(1)}, u32[32]{0:T(128)}, u32[]{:S(2)}) copy-start(u32[32]{0:T(128)} %constant.104) | copy-start | bytes 388
  9.1 14.6 %copy-start.3 = (s32[4]{0:T(128)S(1)}, s32[4]{0:T(128)}, u32[]{:S(2)}) copy-start(s32[4]{0:T(128)} %param.9) | copy-start | bytes 52
  16.1 21.7 %all-to-all-start = ((bf16[8,2,18432]{2,1,0:T(2,128)(2,1)}), bf16[8,2,18432]{2,1,0:T(2,128)(2,1)S(1)}, u32[]{:S(2)}, u32[]{:S(2)}) async-start(bf16[8,2,18432]{2,1,0:T(2,128)(2,1)} %reshape.342), calls=%async_computation | async-start | bytes 1179648 | tf_op jit(solution)/shard_map/all_to_all | solution.py:95
  66.3 11.1 %copy-start.4 = (f32[16]{0:T(128)S(1)}, f32[16]{0:T(128)}, u32[]{:S(2)}) copy-start(f32[16]{0:T(128)} %param.11) | copy-start | bytes 196
  72.4 14.4 %all-to-all-start.1 = ((bf16[8,3,4,96,16]{3,4,2,1,0:T(8,128)(2,1)}), bf16[8,3,4,96,16]{3,4,2,1,0:T(8,128)(2,1)S(1)}, u32[]{:S(2)}, u32[]{:S(2)}) async-start(bf16[8,3,4,96,16]{3,4,2,1,0:T(8,128)(2,1)} %constant_dynamic-update-slice_fusion), calls=%async_computation.1 | async-start | bytes 786432 | tf_op jit(solution)/shard_map/all_to_all | solution.py:11
  86.9 1.3 %copy-start.2 = (f32[384]{0:T(512)S(1)}, f32[384]{0:T(512)}, u32[]{:S(2)}) copy-start(f32[384]{0:T(512)} %param.10) | copy-start | bytes 4612
  87.4 1.4 %copy-start.1 = (bf16[3,2,4,4,65]{4,3,2,1,0:T(4,128)(2,1)S(1)}, bf16[3,2,4,4,65]{4,3,2,1,0:T(4,128)(2,1)}, u32[]{:S(2)}) copy-start(bf16[3,2,4,4,65]{4,3,2,1,0:T(4,128)(2,1)} %param.6) | copy-start | bytes 37444
  88.8 8.1 %collective-permute-start = (bf16[3,2,2,4,65]{4,2,1,0,3:T(2,128)(2,1)S(1)}, bf16[3,2,2,4,65]{4,2,1,0,3:T(2,128)(2,1)S(1)}, u32[]{:S(2)}, u32[]{:S(2)}) collective-permute-start(bf16[3,2,2,4,65]{4,2,1,0,3:T(2,128)(2,1)S(1)} %get-tuple-element.27), channel_id=1, source_target_pairs={{0,1},{1,2},{2,3},{4,5},{5,6},{6,7},{8,9},{9,10},{10,11},{12,13},{... | collective-permute-start | bytes 18728 | tf_op jit(solution)/shard_map/ppermute | solution.py:24
  95.0 5.0 %collective-permute-start.1 = (bf16[3,2,2,4,65]{4,2,1,0,3:T(2,128)(2,1)S(1)}, bf16[3,2,2,4,65]{4,2,1,0,3:T(2,128)(2,1)S(1)}, u32[]{:S(2)}, u32[]{:S(2)}) collective-permute-start(bf16[3,2,2,4,65]{4,2,1,0,3:T(2,128)(2,1)S(1)} %get-tuple-element.28), channel_id=1, source_target_pairs={{1,0},{2,1},{3,2},{5,4},{6,5},{7,6},{9,8},{10,9},{11,10},{13,12},{... | collective-permute-start | bytes 18728 | tf_op jit(solution)/shard_map/ppermute | solution.py:26
